TPU v7x, 256 devices: a whole 4x4x8 slice. The times are simulated.
256 devices in a mesh: dp: 32 (over x, z_lo, y), tensor: 8 (over z_hi, core).
Axes of the slice: x: 4, y: 4, z: 8 (z_hi: 4, z_lo: 2; z = z_hi * 2 + z_lo), core: 2. Of those that a mesh axis runs over, the one named last changes fastest.
Arguments:
- gradient: bfloat16 [2, 2048, 16384], P(None, 'dp', 'tensor'), may hold values from -1000 to 1000
- master: float32 [2, 2048, 16384], P(None, 'dp', 'tensor'), may hold values from -0.046875 to 0.046875
- first_moment: float32 [2, 2048, 16384], P(None, 'dp', 'tensor'), may hold values from -3 to 3
- second_moment: float32 [2, 2048, 16384], P(None, 'dp', 'tensor'), may hold values from 0.05 to 1
- residual: bfloat16 [8192, 16384], P('dp', 'tensor'), may hold values from -1500 to 1500
- norm_gain: float32 [16384], replicated, may hold values from 0.5 to 2
- queries: bfloat16 [8192, 128, 128], P('dp', 'tensor'), may hold values from -170 to 170
- layer_cache: bfloat16 [8192, 2, 8, 32, 128], P('dp', None, 'tensor'), may hold values from -4.5 to 4.5
- fresh_entries: bfloat16 [8192, 2, 8, 128], P('dp', None, 'tensor'), may hold values from -6 to 6
- lengths: int32 [8192], P('dp'), may hold values from 2 to 32, as said below
- shard_table: int32 [32], replicated, may hold values from 0 to 31, each once
Outputs:
- new_first: float32 [2, 2048, 16384], P(None, 'dp', 'tensor')
- new_second: float32 [2, 2048, 16384], P(None, 'dp', 'tensor')
- attended: bfloat16 [8192, 128, 128], P('dp', 'tensor')
- activated: bfloat16 [8192, 2048], P('dp', 'tensor')
Inputs may be any that keep to these rules, and one draw needn't show every extreme that they name: `lengths`: every row has 2 or more valid positions, and in each rollout group's rows one row has all 32. `shard_table`: A permutation of the learner shards.
All inputs are finite; a program needn't handle non-finite values.
Results may differ from a plain program's by a relative error of at most 0.0072.
Values may be sent and summed in bfloat16 or wider, within the bound.
A program may use at most 128 MiB of HBM per device.

v0:
```python
import math
import jax
import jax.numpy as jnp
from jax import lax
from jax.sharding import PartitionSpec as P

LEARN_RATE = 0.001
CLIP_LEVEL = 0.5
CLIP_EPSILON = 1e-06
FIRST_DECAY = 0.9
SECOND_DECAY = 0.95
FIRST_CORRECTION = 1.0 - 0.9**10
SECOND_CORRECTION = 1.0 - 0.95**10
ADAM_EPSILON = 1e-08
NORM_EPSILON = 1e-05


def adam_update(gradient, master, first_moment, second_moment):
    entry_count = (
        gradient.shape[0]
        * gradient.shape[1]
        * lax.axis_size("dp")
        * gradient.shape[2]
        * lax.axis_size("tensor")
    )
    gradient_wide = gradient.astype(jnp.float32)
    local_sum = jnp.sum(gradient_wide * gradient_wide)
    total_sum = lax.psum(local_sum, ("dp", "tensor"))
    clip_limit = CLIP_LEVEL * math.sqrt(entry_count)
    clip_factor = jnp.minimum(1.0, clip_limit / (jnp.sqrt(total_sum) + CLIP_EPSILON))
    clipped = gradient_wide * clip_factor
    new_first = FIRST_DECAY * first_moment + (1.0 - FIRST_DECAY) * clipped
    new_second = SECOND_DECAY * second_moment + (1.0 - SECOND_DECAY) * clipped * clipped
    adam_step = (
        new_first / FIRST_CORRECTION / (jnp.sqrt(new_second / SECOND_CORRECTION) + ADAM_EPSILON)
    )
    fresh_weight = (master - LEARN_RATE * adam_step).astype(jnp.bfloat16)
    return (new_first, new_second, fresh_weight)


def attend(queries, layer_cache, fresh_entries, lengths):
    row_count, head_count, head_width = queries.shape
    group_count = layer_cache.shape[2]
    per_group = head_count // group_count
    score_scale = 1.0 / math.sqrt(head_width)
    grouped = queries.reshape(row_count, group_count, per_group, head_width)
    cached_keys = layer_cache[:, 0]
    cached_values = layer_cache[:, 1]
    scores = (
        jnp.einsum("rghd,rgpd->rghp", grouped, cached_keys, preferred_element_type=jnp.float32)
        * score_scale
    )
    own_score = (
        jnp.einsum(
            "rghd,rgd->rgh", grouped, fresh_entries[:, 0], preferred_element_type=jnp.float32
        )
        * score_scale
    )
    positions = lax.broadcasted_iota(jnp.int32, (row_count, 1, 1, cached_keys.shape[2]), 3)
    in_range = positions < lengths[:, None, None, None]
    scores = jnp.where(in_range, scores, -jnp.inf)
    row_peak = jnp.maximum(jnp.max(scores, axis=3), own_score)
    cached_exp = jnp.exp(scores - row_peak[..., None])
    own_exp = jnp.exp(own_score - row_peak)
    denominator = jnp.sum(cached_exp, axis=3) + own_exp
    cached_prob = (cached_exp / denominator[..., None]).astype(jnp.bfloat16)
    own_prob = (own_exp / denominator).astype(jnp.bfloat16)
    combined = jnp.einsum(
        "rghp,rgpd->rghd", cached_prob, cached_values, preferred_element_type=jnp.float32
    )
    combined = (
        combined
        + own_prob[..., None].astype(jnp.float32)
        * fresh_entries[:, 1].astype(jnp.float32)[:, :, None, :]
    )
    return combined.reshape(row_count, head_count, head_width).astype(jnp.bfloat16)


def per_device(
    gradient,
    master,
    first_moment,
    second_moment,
    residual,
    norm_gain,
    queries,
    layer_cache,
    fresh_entries,
    lengths,
    shard_table,
):
    new_first, new_second, fresh_weight = adam_update(gradient, master, first_moment, second_moment)
    row_count = residual.shape[0]
    shard_count = lax.axis_size("dp")
    rank_count = lax.axis_size("tensor")
    unit_block = fresh_weight.shape[1] // rank_count
    gathered = lax.all_gather(residual, "tensor", axis=1, tiled=True)
    gathered_wide = gathered.astype(jnp.float32)
    mean_square = jnp.mean(gathered_wide * gathered_wide, axis=1, keepdims=True)
    normed = (gathered_wide * lax.rsqrt(mean_square + NORM_EPSILON) * norm_gain).astype(
        jnp.bfloat16
    )
    regrouped = lax.all_to_all(fresh_weight, "tensor", split_axis=1, concat_axis=2, tiled=True)
    projected = jnp.einsum(
        "xk,cuk->xcu",
        normed,
        lax.all_gather(regrouped, "dp", axis=1, tiled=True),
        preferred_element_type=jnp.float32,
    )
    projected = projected.reshape(row_count, 2, shard_count, unit_block)
    hidden = jax.nn.silu(projected[:, 0]) * projected[:, 1]
    ordered = jnp.take(hidden, shard_table, axis=1)
    activated = ordered.reshape(row_count, shard_count * unit_block).astype(jnp.bfloat16)
    attended = attend(queries, layer_cache, fresh_entries, lengths)
    return (new_first, new_second, attended, activated)


def solution(mesh):
    return jax.shard_map(
        per_device,
        mesh=mesh,
        in_specs=(
            P(None, "dp", "tensor"),
            P(None, "dp", "tensor"),
            P(None, "dp", "tensor"),
            P(None, "dp", "tensor"),
            P("dp", "tensor"),
            P(),
            P("dp", "tensor", None),
            P("dp", None, "tensor", None, None),
            P("dp", None, "tensor", None),
            P("dp"),
            P(),
        ),
        out_specs=(
            P(None, "dp", "tensor"),
            P(None, "dp", "tensor"),
            P("dp", "tensor", None),
            P("dp", "tensor"),
        ),
        check_vma=False,
    )
```

profile of v0, /device:TPU:64, one launch (start us, length us, event | category | flops | bytes accessed | tf_op | source)
XLA Modules:
  0.0 359.4 jit_solution(8791076577248445641)
XLA Ops:
  7.2 0.0 copy-start
  7.2 0.0 copy-start.1
  7.2 0.0 all-gather.3.cloned.1.call-start
  7.2 0.7 all-gather.3.cloned.1.call-update
  7.9 0.0 all-gather.5.cloned.1.call-start
  8.0 1.9 fusion.23
  9.9 110.7 %psum.7 = f32[]{:T(128)} all-reduce(f32[]{:T(128)} %fusion.23), channel_id=1, replica_groups=mesh['dp'=32,'tensor'=8] {'dp','tensor'}, use_global_device_ids=true, to_apply=%region_1.0 | all-reduce | flops 1 | bytes 8 | tf_op jit(solution)/shard_map/psum | solution.py:28
  121.3 0.0 copy-done.1
  121.3 3.8 %subtract_convert_fusion = (bf16[2,64,2048]{2,1,0:T(8,128)(2,1)S(1)}, f32[2,64,2048]{2,1,0:T(8,128)}, f32[2,64,2048]{2,1,0:T(8,128)}) fusion(f32[2,64,2048]{2,1,0:T(8,128)S(1)} %copy-done.1, f32[]{:T(128)S(6)} %min_shard_map.3, bf16[2,64,2048]{2,1,0:T(8,128)(2,1)} %param.11, f32[2,64,2048]{2,1,0:T(8,128)} %param.14, f32[2,64,2048]{2,1,0:T(8,128)} %param.13), kind=kLoop, calls=%fused_computation.30 | loop fusion | flops 4194304 | bytes 6291460 | tf_op jit(solution)/shard_map/convert_element_type | solution.py:37
  125.1 0.5 copy.36
  125.7 21.1 %all_to_all.18 = bf16[2,64,2048]{2,0,1:T(2,128)(2,1)S(1)} all-to-all(bf16[2,64,2048]{2,0,1:T(2,128)(2,1)S(1)} %copy.36), channel_id=1, replica_groups=mesh['dp'=32,'tensor'=8] {'tensor'}, dimensions={1} | all-to-all | bytes 1048576 | tf_op jit(solution)/shard_map/all_to_all | solution.py:103
  146.8 1.0 copy.37
  147.8 0.0 all-gather.5.cloned.1.call-update
  147.8 0.0 copy-done.3
  147.9 0.2 fusion.40
  148.1 0.1 broadcast_in_dim.37
  148.2 0.1 broadcast_in_dim.38
  148.3 0.0 copy-done.4
  148.3 0.1 iota_compare_fusion
  148.4 0.7 fusion.32
  149.1 3.1 fusion.14
  152.2 1.3 fusion.15
  153.5 0.1 fusion.35
  153.6 0.0 copy-done.2
  153.6 3.7 %add_convert_fusion = bf16[256,16,128]{2,1,0:T(8,128)(2,1)} fusion(bf16[256,2,1,32,128]{4,3,2,1,0:T(8,128)(2,1)S(1)} %copy-done.2, f32[256,16,32]{2,1,0:T(8,128)S(1)} %get-tuple-element.24, f32[256,128]{1,0:T(8,128)S(1)} %bitcast.54, f32[256,16]{1,0:T(8,128)S(1)} %get-tuple-element.20, f32[256,16]{1,0:T(8,128)S(1)} %get-tuple-element.19, ...), kind=kOutput, calls=%fused_computation.14 | convolution fusion | flops 35782656 | bytes 5799936 | tf_op jit(solution)/shard_map/rghp,rgpd->rghd/dot_general | solution.py:68
  157.3 5.2 %fusion = f32[256]{0:T(256)S(1)} fusion(bf16[256,16384]{1,0:T(8,128)(2,1)} %all-gather.3.cloned.1.call-done), kind=kLoop, calls=%fused_computation.3 | loop fusion | flops 12582656 | bytes 8389632 | tf_op jit(solution)/shard_map/reduce_sum | solution.py:99
  162.5 176.5 %all-gather.5.cloned.1.call-done = bf16[2,256,16384]{2,1,0:T(8,128)(2,1)} async-done(((bf16[2,8,16384]{2,1,0:T(8,128)(2,1)}), bf16[2,256,16384]{2,1,0:T(8,128)(2,1)}) %all-gather.5.cloned.1.call-update) | async-done | bytes 16777232 | tf_op jit(solution)/shard_map/all_gather | solution.py:107
  339.0 12.0 %fusion.19 = f32[256,2,32,8]{0,3,2,1:T(8,128)S(1)} fusion(bf16[2,256,16384]{2,1,0:T(8,128)(2,1)} %all-gather.5.cloned.1.call-done, bf16[256,16384]{1,0:T(8,128)(2,1)} %all-gather.3.cloned.1.call-done, f32[16384]{0:T(1024)S(1)} %copy-done.5, f32[256]{0:T(256)S(1)} %add_rsqrt_fusion), kind=kOutput, calls=%fused_computation.26 | convolution fusion | flops 4311744512 | bytes 25756672 | tf_op jit(solution)/shard_map/xk,cuk->xcu/dot_general | solution.py:104
  351.0 0.1 fusion.30
  351.1 0.6 gather_fusion
  351.7 0.1 fusion.31
  351.8 0.8 copy.38
  (15 shorter events, 0.1 us)
Async XLA Ops:
  7.2 141.2 %copy-start = (bf16[256,16,128]{2,1,0:T(8,128)(2,1)S(1)}, bf16[256,16,128]{2,1,0:T(8,128)(2,1)}, u32[]{:S(2)}) copy-start(bf16[256,16,128]{2,1,0:T(8,128)(2,1)} %param.17) | copy-start | bytes 3145732
  7.2 114.1 %copy-start.1 = (f32[2,64,2048]{2,1,0:T(8,128)S(1)}, f32[2,64,2048]{2,1,0:T(8,128)}, u32[]{:S(2)}) copy-start(f32[2,64,2048]{2,1,0:T(8,128)} %param.12) | copy-start | bytes 3145732
  7.2 150.1 %all-gather.3.cloned.1.call-start = ((), (), s32[]{:S(2)}) async-start(), calls=%async_computation.1 | async-start | bytes 9437184 | tf_op jit(solution)/shard_map/all_gather | solution.py:97
  7.9 331.0 %all-gather.5.cloned.1.call-start = ((), (), s32[]{:S(2)}) async-start(), calls=%async_computation.2 | async-start | bytes 17301504 | tf_op jit(solution)/shard_map/all_gather | solution.py:107
  125.1 22.7 %copy-start.3 = (bf16[256,2,1,128]{3,1,2,0:T(2,128)(2,1)S(1)}, bf16[256,2,1,128]{3,1,2,0:T(2,128)(2,1)}, u32[]{:S(2)}) copy-start(bf16[256,2,1,128]{3,1,2,0:T(2,128)(2,1)} %param.19) | copy-start | bytes 393220
  125.1 22.9 %copy-start.6 = (s32[32]{0:T(128)S(1)}, s32[32]{0:T(128)}, u32[]{:S(2)}) copy-start(s32[32]{0:T(128)} %param.21) | copy-start | bytes 388
  125.1 23.2 %copy-start.4 = (s32[256]{0:T(256)S(1)}, s32[256]{0:T(256)}, u32[]{:S(2)}) copy-start(s32[256]{0:T(256)} %param.20) | copy-start | bytes 3076
  149.1 4.5 %copy-start.2 = (bf16[256,2,1,32,128]{4,3,2,1,0:T(8,128)(2,1)S(1)}, bf16[256,2,1,32,128]{4,3,2,1,0:T(8,128)(2,1)}, u32[]{:S(2)}) copy-start(bf16[256,2,1,32,128]{4,3,2,1,0:T(8,128)(2,1)} %param.18) | copy-start | bytes 12582916
  157.3 181.7 %copy-start.5 = (f32[16384]{0:T(1024)S(1)}, f32[16384]{0:T(1024)}, u32[]{:S(2)}) copy-start(f32[16384]{0:T(1024)} %param.16) | copy-start | bytes 196612
Sparse Core Ops, SparseCore 0:
  9.9 90.7 all-gather.2
  148.0 190.9 all-gather.4
where the time goes:
time: 360 us; the launch traced here: 359 us
  waiting for transfers between devices  177 us (49%)
  blocking collectives  132 us (37%)
  matrix products  19.5 us (5%)
  between operations  15 us (4%)
  other arithmetic  12.8 us (4%)
    all_gather x1, waiting for transfers between devices, per_device(): lax.all_gather(regrouped, 'dp', axis=1, tiled=True)  177 us
    psum x1, blocking collectives, adam_update(): total_sum = lax.psum(local_sum, ('dp', 'tensor'))  111 us
    all_to_all x1, blocking collectives, per_device(): lax.all_to_all(fresh_weight, 'tensor', split_axis=1, concat_axis=2, tiled...  21.1 us
    dot_general x1, matrix products, per_device(): jnp.einsum('xk,cuk->xcu', normed, lax.all_gather(regrouped, 'dp', axis=1,...  12 us
  transfers between devices with their start and end apart: 2, of which 1 were waited for; matrix products, arithmetic and copies ran while one was open for 6% of the time, Pallas kernels for 0%

commit v1 on v0

--- a/solution.py
+++ b/solution.py
@@ -13,6 +13,13 @@
 SECOND_CORRECTION = 1.0 - 0.95**10
 ADAM_EPSILON = 1e-08
 NORM_EPSILON = 1e-05
+
+
+def swap_blocks(x, name, split, join):
+    peers = lax.axis_size(name)
+    tiles = jnp.stack(jnp.split(x, peers, axis=split), axis=0)
+    tiles = lax.all_to_all(tiles, name, split_axis=0, concat_axis=0)
+    return jnp.concatenate(tiles, axis=join)
 
 
 def adam_update(gradient, master, first_moment, second_moment):
@@ -100,7 +107,7 @@
     normed = (gathered_wide * lax.rsqrt(mean_square + NORM_EPSILON) * norm_gain).astype(
         jnp.bfloat16
     )
-    regrouped = lax.all_to_all(fresh_weight, "tensor", split_axis=1, concat_axis=2, tiled=True)
+    regrouped = swap_blocks(fresh_weight, "tensor", 1, 2)
     projected = jnp.einsum(
         "xk,cuk->xcu",
         normed,

time: 360 us -> 359 us (level)
  no operation moved by 1% of the time
where the time goes in v1:
time: 359 us
  waiting for transfers between devices  177 us (49%)
  blocking collectives  132 us (37%)
  matrix products  19.5 us (5%)
  between operations  15 us (4%)
  other arithmetic  12.8 us (4%)
    all_gather x1, waiting for transfers between devices, per_device(): lax.all_gather(regrouped, 'dp', axis=1, tiled=True)  177 us
    psum x1, blocking collectives, adam_update(): total_sum = lax.psum(local_sum, ('dp', 'tensor'))  111 us
    all_to_all x1, blocking collectives, swap_blocks(): tiles = lax.all_to_all(tiles, name, split_axis=0, concat_axis=0)  21.1 us
    dot_general x1, matrix products, per_device(): jnp.einsum('xk,cuk->xcu', normed, lax.all_gather(regrouped, 'dp', axis=1,...  12 us
  transfers between devices with their start and end apart: 2, of which 1 were waited for; matrix products, arithmetic and copies ran while one was open for 6% of the time, Pallas kernels for 0%

profile of v1, /device:TPU:64, one launch (start us, length us, event | category | flops | bytes accessed | tf_op | source)
XLA Modules:
  0.0 358.8 jit_solution(10007632531197399855)
XLA Ops:
  7.2 0.0 copy-start
  7.2 0.0 copy-start.1
  7.2 0.0 all-gather.3.cloned.1.call-start
  7.2 0.7 all-gather.3.cloned.1.call-update
  7.9 0.0 all-gather.5.cloned.1.call-start
  8.0 1.9 fusion.23
  9.9 110.7 %psum.7 = f32[]{:T(128)} all-reduce(f32[]{:T(128)} %fusion.23), channel_id=1, replica_groups=mesh['dp'=32,'tensor'=8] {'dp','tensor'}, use_global_device_ids=true, to_apply=%region_1.0 | all-reduce | flops 1 | bytes 8 | tf_op jit(solution)/shard_map/psum | solution.py:35
  121.3 0.0 copy-done.1
  121.3 3.8 %subtract_convert_fusion = (bf16[2,64,2048]{2,1,0:T(8,128)(2,1)S(1)}, f32[2,64,2048]{2,1,0:T(8,128)}, f32[2,64,2048]{2,1,0:T(8,128)}) fusion(f32[2,64,2048]{2,1,0:T(8,128)S(1)} %copy-done.1, f32[]{:T(128)S(6)} %min_shard_map.3, bf16[2,64,2048]{2,1,0:T(8,128)(2,1)} %param.11, f32[2,64,2048]{2,1,0:T(8,128)} %param.14, f32[2,64,2048]{2,1,0:T(8,128)} %param.13), kind=kLoop, calls=%fused_computation.30 | loop fusion | flops 4194304 | bytes 6291460 | tf_op jit(solution)/shard_map/convert_element_type | solution.py:44
  125.2 0.0 copy-start.4
  125.3 21.1 %all_to_all.5 = bf16[8,2,8,2048]{3,2,1,0:T(8,128)(2,1)S(1)} all-to-all(bf16[8,2,8,2048]{3,2,1,0:T(8,128)(2,1)S(1)} %fusion.35), channel_id=1, replica_groups=mesh['dp'=32,'tensor'=8] {'tensor'}, dimensions={0} | all-to-all | bytes 1048576 | tf_op jit(solution)/shard_map/all_to_all | solution.py:21
  146.4 0.9 copy.22
  147.3 0.0 all-gather.5.cloned.1.call-update
  147.3 0.0 copy-done.6
  147.3 0.1 broadcast_in_dim.37
  147.4 0.1 broadcast_in_dim.38
  147.5 0.0 copy-done.3
  147.5 0.2 fusion.48
  147.7 0.0 copy-done.4
  147.8 0.1 iota_compare_fusion
  147.9 0.7 fusion.32
  148.5 3.1 fusion.14
  151.6 1.3 fusion.15
  152.9 0.1 fusion.43
  153.0 3.7 %add_convert_fusion = bf16[256,16,128]{2,1,0:T(8,128)(2,1)} fusion(bf16[256,2,1,32,128]{4,3,2,1,0:T(8,128)(2,1)S(1)} %copy-done.2, f32[256,16,32]{2,1,0:T(8,128)S(1)} %get-tuple-element.16, f32[256,128]{1,0:T(8,128)S(1)} %bitcast.84, f32[256,16]{1,0:T(8,128)S(1)} %get-tuple-element.12, f32[256,16]{1,0:T(8,128)S(1)} %get-tuple-element.11, ...), kind=kOutput, calls=%fused_computation.14 | convolution fusion | flops 35782656 | bytes 5799936 | tf_op jit(solution)/shard_map/rghp,rgpd->rghd/dot_general | solution.py:75
  156.7 5.2 %fusion = f32[256]{0:T(256)S(1)} fusion(bf16[256,16384]{1,0:T(8,128)(2,1)} %all-gather.3.cloned.1.call-done), kind=kLoop, calls=%fused_computation.3 | loop fusion | flops 12582656 | bytes 8389632 | tf_op jit(solution)/shard_map/reduce_sum | solution.py:106
  161.9 176.5 %all-gather.5.cloned.1.call-done = bf16[2,256,16384]{2,1,0:T(8,128)(2,1)} async-done(((bf16[2,8,16384]{2,1,0:T(8,128)(2,1)}), bf16[2,256,16384]{2,1,0:T(8,128)(2,1)}) %all-gather.5.cloned.1.call-update) | async-done | bytes 16777232 | tf_op jit(solution)/shard_map/all_gather | solution.py:114
  338.4 12.0 %fusion.19 = f32[256,2,32,8]{0,3,2,1:T(8,128)S(1)} fusion(bf16[2,256,16384]{2,1,0:T(8,128)(2,1)} %all-gather.5.cloned.1.call-done, bf16[256,16384]{1,0:T(8,128)(2,1)} %all-gather.3.cloned.1.call-done, f32[16384]{0:T(1024)S(1)} %copy-done.5, f32[256]{0:T(256)S(1)} %add_rsqrt_fusion), kind=kOutput, calls=%fused_computation.26 | convolution fusion | flops 4311744512 | bytes 25756672 | tf_op jit(solution)/shard_map/xk,cuk->xcu/dot_general | solution.py:111
  350.5 0.1 fusion.30
  350.5 0.6 gather_fusion
  351.1 0.1 fusion.31
  351.2 0.8 copy.23
  (22 shorter events, 0.1 us)
Async XLA Ops:
  7.2 140.7 %copy-start = (bf16[256,16,128]{2,1,0:T(8,128)(2,1)S(1)}, bf16[256,16,128]{2,1,0:T(8,128)(2,1)}, u32[]{:S(2)}) copy-start(bf16[256,16,128]{2,1,0:T(8,128)(2,1)} %param.17) | copy-start | bytes 3145732
  7.2 114.1 %copy-start.1 = (f32[2,64,2048]{2,1,0:T(8,128)S(1)}, f32[2,64,2048]{2,1,0:T(8,128)}, u32[]{:S(2)}) copy-start(f32[2,64,2048]{2,1,0:T(8,128)} %param.12) | copy-start | bytes 3145732
  7.2 149.5 %all-gather.3.cloned.1.call-start = ((), (), s32[]{:S(2)}) async-start(), calls=%async_computation.1 | async-start | bytes 9437184 | tf_op jit(solution)/shard_map/all_gather | solution.py:104
  7.9 330.5 %all-gather.5.cloned.1.call-start = ((), (), s32[]{:S(2)}) async-start(), calls=%async_computation.2 | async-start | bytes 17301504 | tf_op jit(solution)/shard_map/all_gather | solution.py:114
  125.1 22.2 %copy-start.6 = (s32[32]{0:T(128)S(1)}, s32[32]{0:T(128)}, u32[]{:S(2)}) copy-start(s32[32]{0:T(128)} %param.21) | copy-start | bytes 388
  125.1 22.4 %copy-start.3 = (bf16[256,2,1,128]{3,1,2,0:T(2,128)(2,1)S(1)}, bf16[256,2,1,128]{3,1,2,0:T(2,128)(2,1)}, u32[]{:S(2)}) copy-start(bf16[256,2,1,128]{3,1,2,0:T(2,128)(2,1)} %param.19) | copy-start | bytes 393220
  125.2 22.6 %copy-start.4 = (s32[256]{0:T(256)S(1)}, s32[256]{0:T(256)}, u32[]{:S(2)}) copy-start(s32[256]{0:T(256)} %param.20) | copy-start | bytes 3076
  148.5 4.5 %copy-start.2 = (bf16[256,2,1,32,128]{4,3,2,1,0:T(8,128)(2,1)S(1)}, bf16[256,2,1,32,128]{4,3,2,1,0:T(8,128)(2,1)}, u32[]{:S(2)}) copy-start(bf16[256,2,1,32,128]{4,3,2,1,0:T(8,128)(2,1)} %param.18) | copy-start | bytes 12582916
  156.7 181.7 %copy-start.5 = (f32[16384]{0:T(1024)S(1)}, f32[16384]{0:T(1024)}, u32[]{:S(2)}) copy-start(f32[16384]{0:T(1024)} %param.16) | copy-start | bytes 196612
Sparse Core Ops, SparseCore 0:
  9.9 90.7 all-gather.2
  147.4 190.9 all-gather.4
